TPU v7x, 256 devices: a whole 4x4x8 slice. The times are simulated.
256 devices in a mesh: batch: 8 (over x, core), hidden: 4 (over z_hi), solver: 8 (over z_lo, y).
Axes of the slice: x: 4, y: 4, z: 8 (z_hi: 4, z_lo: 2; z = z_hi * 2 + z_lo), core: 2. Of those that a mesh axis runs over, the one named last changes fastest.
Arguments:
- activations: bfloat16 [2048, 4096], P('batch', ('hidden', 'solver')), may hold values from -16 to 16, as said below
- cotangent: bfloat16 [8192, 2048], P(('hidden', 'solver'), 'batch'), may hold values from -0.13183594 to 0.13183594
- weight: bfloat16 [4096, 8192], P(('hidden', 'solver'), 'batch'), may hold values from -0.09375 to 0.09375
- left_old: float32 [4, 8, 1024, 1024], P('hidden', 'batch'), may hold values from -0.001953125 to 2.0019531, as said below
- right_old: float32 [4, 8, 1024, 1024], P('hidden', 'batch'), may hold values from -0.001953125 to 2.0019531, as said below
Outputs:
- first_out: bfloat16 [8192, 2048], P(('hidden', 'solver'), 'batch')
- new_left: float32 [4, 8, 1024, 1024], P('hidden', 'batch', 'solver')
- new_right: float32 [4, 8, 1024, 1024], P('hidden', 'batch', 'solver')
- direction: float32 [4096, 8192], P(('hidden', 'solver'), 'batch')
- second_out: bfloat16 [8192, 2048], P(('hidden', 'solver'), 'batch')
Inputs may be any that keep to these rules, and one draw needn't show every extreme that they name: `activations`: in the hidden draw each feature carries its own scale. `left_old`: every block is symmetric, its diagonal is positive and larger than the sum of the magnitudes of the rest of its row. `right_old`: every block is symmetric, its diagonal is positive and larger than the sum of the magnitudes of the rest of its row.
All inputs are finite; a program needn't handle non-finite values. Where the computation divides by a largest or mean magnitude, that divisor is 1e-20 or more.
Results may differ from a plain program's by a relative error of at most 0.017.
Values may be sent and summed in bfloat16 or wider, within the bound.
No kernel may reach another device: no remote copies, remote signals or barrier semaphores. Data moves between devices by JAX's collectives and lax.ppermute only.
A program may use at most 128 MiB of HBM per device.

v0:
```python
import jax
import jax.numpy as jnp
from jax import lax
from jax.sharding import PartitionSpec as P

BLOCK = 1024
STAT_DECAY = 0.8
LEARN_RATE = 0.005
EPSILON = 1e-06


def in_order(blocks, dim):
    blocks = jnp.moveaxis(blocks, 0, dim)
    shape = blocks.shape
    return blocks.reshape(*shape[:dim], shape[dim] * shape[dim + 1], *shape[dim + 2 :])


def sent_to_all(shard, axis):
    copies = jnp.broadcast_to(shard, (lax.axis_size(axis), *shard.shape))
    return lax.all_to_all(copies, axis, split_axis=0, concat_axis=0, tiled=True)


def gather_directly(shard, axis, dim):
    return in_order(sent_to_all(shard, axis), dim)


def cut_along(shard, dim, peers):
    before, after = (shard.shape[:dim], shard.shape[dim + 1 :])
    return jnp.moveaxis(shard.reshape(*before, peers, -1, *after), dim, 0)


def summed_on_arrival(shard, axis, dim):
    blocks = cut_along(shard, dim, lax.axis_size(axis))
    arrived = lax.all_to_all(blocks, axis, split_axis=0, concat_axis=0, tiled=True)
    return arrived.astype(jnp.float32).sum(axis=0)


def taken_together(shard, axis):
    everything = sent_to_all(shard, axis)
    return jnp.sum(everything, axis=0)


def product(left_mat, right_mat):
    return jnp.einsum("bij,bjk->bik", left_mat, right_mat, preferred_element_type=jnp.float32)


def prepare(factor):
    identity = jnp.eye(BLOCK, dtype=jnp.float32)
    scaled = 2.5 / (jnp.max(jnp.sum(jnp.abs(factor), axis=2), axis=1) + EPSILON)
    moment = scaled[:, None, None] * factor
    newton_step = (5.0 * identity - moment) * 0.25
    return (scaled, moment, newton_step)


def transposed_product(weight_cols, acts):
    return lax.dot_general(
        weight_cols, acts, (((0,), (1,)), ((), ())), preferred_element_type=jnp.float32
    )


def body(activations, cotangent, weight, left_old, right_old):
    rows_here = weight.shape[0]
    nblocks = weight.shape[1] // BLOCK
    weight_rows = gather_directly(weight, "batch", 1)
    gathered = lax.all_gather(activations, ("hidden", "solver"), axis=1, tiled=True)
    weight_cols = lax.all_to_all(
        weight_rows, ("hidden", "solver"), split_axis=1, concat_axis=0, tiled=True
    )
    first_sum = transposed_product(weight_cols, gathered)
    first_out = first_sum.astype(jnp.bfloat16)
    cotangent_all = lax.all_gather(cotangent, ("hidden", "solver"), axis=0, tiled=True)
    grad_local = summed_on_arrival(
        jnp.dot(cotangent_all, activations, preferred_element_type=jnp.float32).astype(
            jnp.bfloat16
        ),
        "batch",
        0,
    ).astype(jnp.bfloat16)
    grad_blocks = grad_local.reshape(nblocks, BLOCK, rows_here)
    grad_full = gather_directly(grad_blocks, "solver", 2)
    gram_left = jnp.einsum("bnm,bnk->bmk", grad_full, grad_full, preferred_element_type=jnp.float32)
    gram_right = jnp.einsum(
        "bnm,bkm->bnk", grad_full, grad_full, preferred_element_type=jnp.float32
    )
    left_all = STAT_DECAY * left_old[0] + (1.0 - STAT_DECAY) / BLOCK * gram_left
    right_all = STAT_DECAY * right_old[0] + (1.0 - STAT_DECAY) / BLOCK * gram_right
    first_row = lax.axis_index("solver") * rows_here
    new_left = lax.dynamic_slice_in_dim(left_all, first_row, rows_here, 1)[None]
    new_right = lax.dynamic_slice_in_dim(right_all, first_row, rows_here, 1)[None]
    scale_left, moment_left, step_left = prepare(left_all)
    own_rows = lax.dynamic_slice_in_dim(step_left, first_row, rows_here, 1)
    power_rows = product(
        product(product(product(own_rows, step_left), step_left), step_left), moment_left
    )
    row_index = lax.broadcasted_iota(jnp.int32, (rows_here, BLOCK), 0) + first_row
    col_index = lax.broadcasted_iota(jnp.int32, (rows_here, BLOCK), 1)
    eye_rows = (row_index == col_index).astype(jnp.float32)
    next_rows = (5.0 * eye_rows - power_rows) * 0.25
    root_rows = (scale_left**0.25)[:, None, None] * product(next_rows, step_left)
    grad_float = grad_full.astype(jnp.float32)
    mixed_rows = jnp.einsum(
        "brm,bnm->brn", root_rows, grad_float, preferred_element_type=jnp.float32
    )
    scale_right, moment_right, step_right = prepare(right_all)
    turned = product(mixed_rows, step_right)
    power_right = product(
        product(product(product(product(turned, step_right), step_right), step_right), step_right),
        moment_right,
    )
    update = (scale_right**0.25)[:, None, None] * ((5.0 * turned - power_right) * 0.25)
    squares = taken_together(jnp.sum(update * update, axis=(1, 2)), "solver")
    spread = jnp.sqrt(squares / (BLOCK * BLOCK) + EPSILON)
    scaled_update = update / spread[:, None, None]
    direction = jnp.transpose(scaled_update, (1, 0, 2)).reshape(rows_here, nblocks * BLOCK)
    new_weight = (weight.astype(jnp.float32) - LEARN_RATE * direction).astype(jnp.bfloat16)
    new_rows = gather_directly(new_weight, "batch", 1)
    new_cols = lax.all_to_all(
        new_rows, ("hidden", "solver"), split_axis=1, concat_axis=0, tiled=True
    )
    second_sum = transposed_product(new_cols, gathered)
    second_out = second_sum.astype(jnp.bfloat16)
    return (first_out, new_left, new_right, direction, second_out)


def solution(mesh):
    in_specs = (
        P("batch", ("hidden", "solver")),
        P(("hidden", "solver"), "batch"),
        P(("hidden", "solver"), "batch"),
        P("hidden", "batch", None, None),
        P("hidden", "batch", None, None),
    )
    out_specs = (
        P(("hidden", "solver"), "batch"),
        P("hidden", "batch", "solver", None),
        P("hidden", "batch", "solver", None),
        P(("hidden", "solver"), "batch"),
        P(("hidden", "solver"), "batch"),
    )
    return jax.shard_map(body, mesh=mesh, in_specs=in_specs, out_specs=out_specs, check_vma=False)
```

profile of v0, /device:TPU:24, one launch (start us, length us, event | category | flops | bytes accessed | tf_op | source)
XLA Modules:
  0.0 407.6 jit_solution(7480275849484787042)
XLA Ops:
  7.2 0.0 all-gather.5.cloned.1.call-start
  7.2 0.7 all-gather.5.cloned.1.call-update
  7.9 85.3 %all-gather.5.cloned.1.call-done = bf16[8192,256]{1,0:T(8,128)(2,1)} async-done(((bf16[256,256]{1,0:T(8,128)(2,1)}), bf16[8192,256]{1,0:T(8,128)(2,1)}) %all-gather.5.cloned.1.call-update) | async-done | bytes 4194320 | tf_op jit(solution)/shard_map/all_gather | solution.py:71
  93.2 3.4 convolution_convert_fusion
  96.7 31.6 %all_to_all.64 = bf16[8,1024,128]{2,1,0:T(8,128)(2,1)S(1)} all-to-all(bf16[8,1024,128]{2,1,0:T(8,128)(2,1)S(1)} %bitcast.48), channel_id=1, replica_groups=mesh['batch'=8,'hidden'=4,'solver'=8] {'batch'}, dimensions={0} | all-to-all | bytes 4194304 | tf_op jit(solution)/shard_map/all_to_all | solution.py:34
  128.3 0.4 reduce_sum.48
  128.7 1.6 broadcast_in_dim.13
  130.3 6.3 %all-to-all-start.3 = ((bf16[8,1,1024,128]{3,2,1,0:T(8,128)(2,1)}), bf16[8,1,1024,128]{3,2,1,0:T(8,128)(2,1)S(1)}, u32[]{:S(2)}, u32[]{:S(2)}) async-start(bf16[8,1,1024,128]{3,2,1,0:T(8,128)(2,1)} %broadcast_in_dim.13), calls=%async_computation.3 | async-start | bytes 4194304 | tf_op jit(solution)/shard_map/all_to_all | solution.py:20
  136.6 0.2 copy.41
  136.8 5.4 %copy.43 = f32[1,1,1024,1024]{2,3,1,0:T(8,128)} copy(f32[1,1,1024,1024]{3,2,1,0:T(8,128)} %param.8) | data formatting | bytes 8388608 | tf_op args[3]
  142.2 5.3 %copy.47 = f32[1,1,1024,1024]{2,3,1,0:T(8,128)} copy(f32[1,1,1024,1024]{3,2,1,0:T(8,128)} %param.9) | data formatting | bytes 8388608 | tf_op args[4]
  147.5 13.4 %all-to-all-done.3 = bf16[8,1,1024,128]{3,2,1,0:T(8,128)(2,1)S(1)} async-done(((bf16[8,1,1024,128]{3,2,1,0:T(8,128)(2,1)}), bf16[8,1,1024,128]{3,2,1,0:T(8,128)(2,1)S(1)}, u32[]{:S(2)}, u32[]{:S(2)}) %all-to-all-start.3) | async-done | bytes 2097184 | tf_op jit(solution)/shard_map/all_to_all | solution.py:20
  160.9 1.8 broadcast_in_dim.12
  162.8 4.5 %all-to-all-start = ((bf16[8,128,1024]{1,2,0:T(8,128)(2,1)}), bf16[8,128,1024]{1,2,0:T(8,128)(2,1)}, u32[]{:S(2)}, u32[]{:S(2)}) async-start(bf16[8,128,1024]{1,2,0:T(8,128)(2,1)} %broadcast_in_dim.12), calls=%async_computation | async-start | bytes 4194304 | tf_op jit(solution)/shard_map/all_to_all | solution.py:20
  167.3 2.6 copy.45
  170.0 8.1 %abs_reduce_fusion.1 = (f32[1024]{0:T(1024)S(1)}, f32[1024,1024]{0,1:T(8,128)}) fusion(bf16[1024,1024]{0,1:T(8,128)(2,1)} %bitcast.51, f32[1,1,1024,1024]{2,3,1,0:T(8,128)} %copy.43), kind=kOutput, calls=%fused_computation.10 | convolution fusion | flops 2152725504 | bytes 10489856 | tf_op jit(solution)/shard_map/bnm,bnk->bmk/dot_general | solution.py:81
  178.1 0.6 reduce_max.18
  179.4 3.0 fusion
  182.4 0.4 copy-done.1
  182.8 6.8 %abs_reduce_fusion = (f32[1024]{0:T(1024)S(1)}, f32[1024,1024]{0,1:T(8,128)}) fusion(bf16[8,1,1024,128]{3,2,1,0:T(8,128)(2,1)} %copy-done, f32[1,1,1024,1024]{2,3,1,0:T(8,128)S(1)} %copy-done.1), kind=kOutput, calls=%fused_computation.8 | convolution fusion | flops 2152725504 | bytes 10489856 | tf_op jit(solution)/shard_map/bnm,bkm->bnk/dot_general | solution.py:82
  189.6 0.6 reduce_max.19
  190.9 1.5 fusion.45
  192.5 5.1 %fusion.29 = bf16[128,1024]{1,0:T(8,128)(2,1)S(1)} fusion(f32[1024,1024]{0,1:T(8,128)} %get-tuple-element.10, f32[]{:T(128)S(6)} %div.20, bf16[128,1024]{1,0:T(8,128)(2,1)S(1)} %fusion.45, s32[128]{0:T(128)S(1)} %iota_add_fusion), kind=kOutput, calls=%fused_computation.23 | convolution fusion | flops 543817728 | bytes 4719108 | tf_op jit(solution)/shard_map/bij,bjk->bik/dot_general | solution.py:44
  197.6 3.3 fusion.48
  201.0 3.0 fusion.43
  204.1 3.0 fusion.41
  207.1 5.0 %fusion.34 = bf16[128,1024]{1,0:T(8,128)(2,1)S(1)} fusion(bf16[128,1024]{1,0:T(8,128)(2,1)S(1)} %fusion.41, f32[1024,1024]{0,1:T(8,128)} %get-tuple-element.8, f32[]{:T(128)S(6)} %div.21), kind=kOutput, calls=%fused_computation.25 | convolution fusion | flops 547356672 | bytes 4718596 | tf_op jit(solution)/shard_map/bij,bjk->bik/dot_general | solution.py:44
  212.1 5.7 %multiply_reduce_fusion = (f32[]{:T(128)}, f32[128,1024]{1,0:T(8,128)S(1)}) fusion(f32[]{:T(128)S(6)} %mul.123, f32[1024,1024]{0,1:T(8,128)} %get-tuple-element.8, f32[]{:T(128)S(6)} %div.21, bf16[128,1024]{1,0:T(8,128)(2,1)S(1)} %fusion.34, f32[128,1024]{1,0:T(8,128)S(1)} %fusion.43), kind=kOutput, calls=%fused_computation.35 | convolution fusion | flops 543817728 | bytes 5505036 | tf_op jit(solution)/shard_map/bij,bjk->bik/dot_general | solution.py:44
  217.8 0.6 broadcast_in_dim.30
  218.4 8.8 %all_to_all.65 = f32[8,1,1]{2,1,0:T(1,128)S(1)} all-to-all(f32[8,1,1]{2,1,0:T(1,128)S(1)} %broadcast_in_dim.30), channel_id=1, replica_groups=mesh['batch'=8,'hidden'=4,'solver'=8] {'solver'}, dimensions={0} | all-to-all | bytes 64 | tf_op jit(solution)/shard_map/all_to_all | solution.py:20
  227.3 7.1 %all-to-all-start.1 = ((bf16[128,32,256]{0,2,1:T(8,128)(2,1)}), bf16[128,32,256]{0,2,1:T(8,128)(2,1)S(1)}, u32[]{:S(2)}, u32[]{:S(2)}) async-start(bf16[128,32,256]{0,2,1:T(8,128)(2,1)} %bitcast.1), calls=%async_computation.1 | async-start | bytes 4194304 | tf_op jit(solution)/shard_map/all_to_all | solution.py:66
  234.3 0.6 reduce_sum.52
  235.7 0.9 subtract_convert_fusion
  236.5 0.2 copy.50
  236.7 47.1 %all-to-all-done.1 = bf16[128,32,256]{0,2,1:T(8,128)(2,1)S(1)} async-done(((bf16[128,32,256]{0,2,1:T(8,128)(2,1)}), bf16[128,32,256]{0,2,1:T(8,128)(2,1)S(1)}, u32[]{:S(2)}, u32[]{:S(2)}) %all-to-all-start.1) | async-done | bytes 2097184 | tf_op jit(solution)/shard_map/all_to_all | solution.py:66
  283.8 1.6 broadcast_in_dim.31
  285.4 4.5 %all-to-all-start.5 = ((bf16[8,128,1024]{1,2,0:T(8,128)(2,1)}), bf16[8,128,1024]{1,2,0:T(8,128)(2,1)}, u32[]{:S(2)}, u32[]{:S(2)}) async-start(bf16[8,128,1024]{1,2,0:T(8,128)(2,1)} %broadcast_in_dim.31), calls=%async_computation.5 | async-start | bytes 4194304 | tf_op jit(solution)/shard_map/all_to_all | solution.py:20
  289.9 0.7 all-gather.3.cloned.1.call-update
  290.6 26.6 %all-to-all-done.5 = bf16[8,128,1024]{1,2,0:T(8,128)(2,1)} async-done(((bf16[8,128,1024]{1,2,0:T(8,128)(2,1)}), bf16[8,128,1024]{1,2,0:T(8,128)(2,1)}, u32[]{:S(2)}, u32[]{:S(2)}) %all-to-all-start.5) | async-done | bytes 2097184 | tf_op jit(solution)/shard_map/all_to_all | solution.py:20
  317.2 5.6 %all-to-all-start.6 = ((bf16[128,32,256]{0,2,1:T(8,128)(2,1)}), bf16[128,32,256]{0,2,1:T(8,128)(2,1)}, u32[]{:S(2)}, u32[]{:S(2)}) async-start(bf16[128,32,256]{0,2,1:T(8,128)(2,1)} %bitcast.16), calls=%async_computation.6 | async-start | bytes 4194304 | tf_op jit(solution)/shard_map/all_to_all | solution.py:117
  322.8 2.9 copy.42
  325.7 61.8 %all-gather.3.cloned.1.call-done = bf16[256,4096]{1,0:T(8,128)(2,1)} async-done(((bf16[256,128]{1,0:T(8,128)(2,1)}), bf16[256,4096]{1,0:T(8,128)(2,1)}) %all-gather.3.cloned.1.call-update) | async-done | bytes 2097168 | tf_op jit(solution)/shard_map/all_gather | solution.py:65
  387.6 3.6 convolution_convert_fusion.2
  391.2 1.3 constant_dynamic-slice_fusion
  392.5 1.0 copy.48
  393.5 1.0 copy.46
  394.5 3.3 copy.51
  397.7 3.0 convolution_convert_fusion.1
  (11 shorter events, 0.1 us)
Async XLA Ops:
  7.2 86.1 %all-gather.5.cloned.1.call-start = ((), (), s32[]{:S(2)}) async-start(), calls=%async_computation.8 | async-start | bytes 4325376 | tf_op jit(solution)/shard_map/all_gather | solution.py:71
  128.3 8.4 %copy-start.3 = (bf16[128,1024]{1,0:T(8,128)(2,1)S(1)}, bf16[128,1024]{1,0:T(8,128)(2,1)}, u32[]{:S(2)}) copy-start(bf16[128,1024]{1,0:T(8,128)(2,1)} %param.7) | copy-start | bytes 786436
  130.3 30.7 %all-to-all-start.3 = ((bf16[8,1,1024,128]{3,2,1,0:T(8,128)(2,1)}), bf16[8,1,1024,128]{3,2,1,0:T(8,128)(2,1)S(1)}, u32[]{:S(2)}, u32[]{:S(2)}) async-start(bf16[8,1,1024,128]{3,2,1,0:T(8,128)(2,1)} %broadcast_in_dim.13), calls=%async_computation.3 | async-start | bytes 4194304 | tf_op jit(solution)/shard_map/all_to_all | solution.py:20
  160.9 9.0 %copy-start = (bf16[8,1,1024,128]{3,2,1,0:T(8,128)(2,1)}, bf16[8,1,1024,128]{3,2,1,0:T(8,128)(2,1)S(1)}, u32[]{:S(2)}) copy-start(bf16[8,1,1024,128]{3,2,1,0:T(8,128)(2,1)S(1)} %all-to-all-done.3) | copy-start | bytes 6291460
  162.8 55.0 %all-to-all-start = ((bf16[8,128,1024]{1,2,0:T(8,128)(2,1)}), bf16[8,128,1024]{1,2,0:T(8,128)(2,1)}, u32[]{:S(2)}, u32[]{:S(2)}) async-start(bf16[8,128,1024]{1,2,0:T(8,128)(2,1)} %broadcast_in_dim.12), calls=%async_computation | async-start | bytes 4194304 | tf_op jit(solution)/shard_map/all_to_all | solution.py:20
  179.4 3.5 copy-start.1
  192.5 5.2 %copy-start.2 = (bf16[1,1024,8,128]{1,3,2,0:T(8,128)(2,1)S(1)}, bf16[1,1024,8,128]{1,3,2,0:T(8,128)(2,1)}, u32[]{:S(2)}) copy-start(bf16[1,1024,8,128]{1,3,2,0:T(8,128)(2,1)} %copy.45) | copy-start | bytes 6291460
  227.3 56.5 %all-to-all-start.1 = ((bf16[128,32,256]{0,2,1:T(8,128)(2,1)}), bf16[128,32,256]{0,2,1:T(8,128)(2,1)S(1)}, u32[]{:S(2)}, u32[]{:S(2)}) async-start(bf16[128,32,256]{0,2,1:T(8,128)(2,1)} %bitcast.1), calls=%async_computation.1 | async-start | bytes 4194304 | tf_op jit(solution)/shard_map/all_to_all | solution.py:66
  285.4 31.8 %all-to-all-start.5 = ((bf16[8,128,1024]{1,2,0:T(8,128)(2,1)}), bf16[8,128,1024]{1,2,0:T(8,128)(2,1)}, u32[]{:S(2)}, u32[]{:S(2)}) async-start(bf16[8,128,1024]{1,2,0:T(8,128)(2,1)} %broadcast_in_dim.31), calls=%async_computation.5 | async-start | bytes 4194304 | tf_op jit(solution)/shard_map/all_to_all | solution.py:20
  289.9 97.7 %all-gather.3.cloned.1.call-start = ((), (), s32[]{:S(2)}) async-start(), calls=%async_computation.7 | async-start | bytes 2162688 | tf_op jit(solution)/shard_map/all_gather | solution.py:65
  317.2 77.3 %all-to-all-start.6 = ((bf16[128,32,256]{0,2,1:T(8,128)(2,1)}), bf16[128,32,256]{0,2,1:T(8,128)(2,1)}, u32[]{:S(2)}, u32[]{:S(2)}) async-start(bf16[128,32,256]{0,2,1:T(8,128)(2,1)} %bitcast.16), calls=%async_computation.6 | async-start | bytes 4194304 | tf_op jit(solution)/shard_map/all_to_all | solution.py:117
Sparse Core Ops, SparseCore 0:
  10.6 82.6 all-gather.4
  293.2 94.3 all-gather.2
where the time goes:
time: 408 us
  waiting for transfers between devices  236 us (58%)
  matrix products  51.7 us (13%)
  blocking collectives  40.4 us (10%)
  local copies, waits for them, and re-layouts  29.3 us (7%)
  starting transfers between devices  28.1 us (7%)
  between operations  16.4 us (4%)
  other arithmetic  6.1 us (1%)
    all_gather x1, waiting for transfers between devices, body(): lax.all_gather(cotangent, ('hidden', 'solver'), axis=0, tiled=True)  85.3 us
    all_gather x1, waiting for transfers between devices, body(): lax.all_gather(activations, ('hidden', 'solver'), axis=1, tiled=True)  61.8 us
    all_to_all x1, waiting for transfers between devices, body(): lax.all_to_all(weight_rows, ('hidden', 'solver'), split_axis=1, concat_ax...  47.1 us
    all_to_all x3, waiting for transfers between devices, sent_to_all(): return lax.all_to_all(copies, axis, split_axis=0, concat_axis=0, tiled=True)  40 us
    all_to_all x1, blocking collectives, summed_on_arrival(): lax.all_to_all(blocks, axis, split_axis=0, concat_axis=0, tiled=True)  31.6 us
    dot_general x6, matrix products, product(): jnp.einsum('bij,bjk->bik', left_mat, right_mat, preferred_element_type=jn...  23.4 us
    all_to_all x3, starting transfers between devices, sent_to_all(): return lax.all_to_all(copies, axis, split_axis=0, concat_axis=0, tiled=True)  15.3 us
    unnamed x11, local copies, waits for them, and re-layouts  11.3 us
  transfers between devices with their start and end apart: 7, of which 5 were waited for; matrix products, arithmetic and copies ran while one was open for 17% of the time, Pallas kernels for 0%

commit v1 on v0

--- a/solution.py
+++ b/solution.py
@@ -68,7 +68,12 @@
     )
     first_sum = transposed_product(weight_cols, gathered)
     first_out = first_sum.astype(jnp.bfloat16)
-    cotangent_all = lax.all_gather(cotangent, ("hidden", "solver"), axis=0, tiled=True)
+    cotangent_all = jnp.concatenate(
+        lax.all_to_all(
+            jnp.stack([cotangent] * lax.axis_size(("hidden", "solver"))), ("hidden", "solver"), 0, 0
+        ),
+        axis=0,
+    )
     grad_local = summed_on_arrival(
         jnp.dot(cotangent_all, activations, preferred_element_type=jnp.float32).astype(
             jnp.bfloat16

time: 408 us -> 426 us (1.044)
  blocking collectives: 40.4 us -> 147 us
  waiting for transfers between devices: 236 us -> 150 us
    all_to_all x0 -> x1, blocking collectives: none -> 107 us  [body(): lax.all_to_all(jnp.stack([cotangent] * lax.axis_size(('hidden', 'solver')...]
    all_gather x1 -> x0, waiting for transfers between devices: 85.3 us -> none  [body(): lax.all_gather(cotangent, ('hidden', 'solver'), axis=0, tiled=True)]
    unnamed x11 -> x13, local copies, waits for them, and re-layouts: 11.3 us -> 11.3 us
  transfers between devices with their start and end apart: 7 -> 6, of which waited for: 5 -> 4; matrix products, arithmetic and copies ran while one was open for 17% -> 17% of each run, Pallas kernels for 0% -> 0%
where the time goes in v1:
time: 426 us; the launch traced here: 425 us
  waiting for transfers between devices  150 us (35%)
  blocking collectives  147 us (35%)
  matrix products  49.5 us (12%)
  local copies, waits for them, and re-layouts  30.7 us (7%)
  starting transfers between devices  25.6 us (6%)
  between operations  16.4 us (4%)
  other arithmetic  6.1 us (1%)
    all_to_all x1, blocking collectives, body(): lax.all_to_all(jnp.stack([cotangent] * lax.axis_size(('hidden', 'solver')...  107 us
    all_gather x1, waiting for transfers between devices, body(): lax.all_gather(activations, ('hidden', 'solver'), axis=1, tiled=True)  61.8 us
    all_to_all x1, waiting for transfers between devices, body(): lax.all_to_all(weight_rows, ('hidden', 'solver'), split_axis=1, concat_ax...  47.3 us
    all_to_all x3, waiting for transfers between devices, sent_to_all(): return lax.all_to_all(copies, axis, split_axis=0, concat_axis=0, tiled=True)  40 us
    all_to_all x1, blocking collectives, summed_on_arrival(): lax.all_to_all(blocks, axis, split_axis=0, concat_axis=0, tiled=True)  31.6 us
    dot_general x6, matrix products, product(): jnp.einsum('bij,bjk->bik', left_mat, right_mat, preferred_element_type=jn...  23.4 us
    all_to_all x3, starting transfers between devices, sent_to_all(): return lax.all_to_all(copies, axis, split_axis=0, concat_axis=0, tiled=True)  13.8 us
    unnamed x13, local copies, waits for them, and re-layouts  11.3 us
  transfers between devices with their start and end apart: 6, of which 4 were waited for; matrix products, arithmetic and copies ran while one was open for 17% of the time, Pallas kernels for 0%

profile of v1, /device:TPU:24, one launch (start us, length us, event | category | flops | bytes accessed | tf_op | source)
XLA Modules:
  0.0 425.4 jit_solution(1706377433920125008)
XLA Ops:
  7.2 1.4 stack.2
  8.6 106.9 %all_to_all.69 = bf16[32,256,256]{2,1,0:T(8,128)(2,1)S(1)} all-to-all(bf16[32,256,256]{2,1,0:T(8,128)(2,1)S(1)} %stack.2), channel_id=1, replica_groups=mesh['batch'=8,'hidden'=4,'solver'=8] {'hidden','solver'}, dimensions={0} | all-to-all | bytes 8388608 | tf_op jit(solution)/shard_map/all_to_all | solution.py:72
  115.4 1.3 convolution_convert_fusion
  116.7 31.6 %all_to_all.70 = bf16[8,1024,128]{2,1,0:T(8,128)(2,1)S(1)} all-to-all(bf16[8,1024,128]{2,1,0:T(8,128)(2,1)S(1)} %bitcast.50), channel_id=1, replica_groups=mesh['batch'=8,'hidden'=4,'solver'=8] {'batch'}, dimensions={0} | all-to-all | bytes 4194304 | tf_op jit(solution)/shard_map/all_to_all | solution.py:34
  148.3 0.4 reduce_sum.48
  148.7 1.6 broadcast_in_dim.13
  150.3 4.8 %all-to-all-start.4 = ((bf16[8,1,1024,128]{3,2,1,0:T(8,128)(2,1)}), bf16[8,1,1024,128]{3,2,1,0:T(8,128)(2,1)S(1)}, u32[]{:S(2)}, u32[]{:S(2)}) async-start(bf16[8,1,1024,128]{3,2,1,0:T(8,128)(2,1)} %broadcast_in_dim.13), calls=%async_computation.4 | async-start | bytes 4194304 | tf_op jit(solution)/shard_map/all_to_all | solution.py:20
  155.2 0.2 copy.41
  155.3 5.4 %copy.43 = f32[1,1,1024,1024]{2,3,1,0:T(8,128)} copy(f32[1,1,1024,1024]{3,2,1,0:T(8,128)} %param.8) | data formatting | bytes 8388608 | tf_op args[3]
  160.7 5.3 %copy.47 = f32[1,1,1024,1024]{2,3,1,0:T(8,128)} copy(f32[1,1,1024,1024]{3,2,1,0:T(8,128)} %param.9) | data formatting | bytes 8388608 | tf_op args[4]
  166.1 13.4 %all-to-all-done.4 = bf16[8,1,1024,128]{3,2,1,0:T(8,128)(2,1)S(1)} async-done(((bf16[8,1,1024,128]{3,2,1,0:T(8,128)(2,1)}), bf16[8,1,1024,128]{3,2,1,0:T(8,128)(2,1)S(1)}, u32[]{:S(2)}, u32[]{:S(2)}) %all-to-all-start.4) | async-done | bytes 2097184 | tf_op jit(solution)/shard_map/all_to_all | solution.py:20
  179.5 1.8 broadcast_in_dim.12
  181.3 4.5 %all-to-all-start = ((bf16[8,128,1024]{1,2,0:T(8,128)(2,1)}), bf16[8,128,1024]{1,2,0:T(8,128)(2,1)}, u32[]{:S(2)}, u32[]{:S(2)}) async-start(bf16[8,128,1024]{1,2,0:T(8,128)(2,1)} %broadcast_in_dim.12), calls=%async_computation | async-start | bytes 4194304 | tf_op jit(solution)/shard_map/all_to_all | solution.py:20
  185.9 2.6 copy.45
  188.5 8.1 %abs_reduce_fusion.1 = (f32[1024]{0:T(1024)S(1)}, f32[1024,1024]{0,1:T(8,128)}) fusion(bf16[1024,1024]{0,1:T(8,128)(2,1)} %bitcast.53, f32[1,1,1024,1024]{2,3,1,0:T(8,128)} %copy.43), kind=kOutput, calls=%fused_computation.10 | convolution fusion | flops 2152725504 | bytes 10489856 | tf_op jit(solution)/shard_map/bnm,bnk->bmk/dot_general | solution.py:86
  196.6 0.6 reduce_max.18
  198.0 3.0 fusion
  201.0 0.4 copy-done.1
  201.4 6.8 %abs_reduce_fusion = (f32[1024]{0:T(1024)S(1)}, f32[1024,1024]{0,1:T(8,128)}) fusion(bf16[8,1,1024,128]{3,2,1,0:T(8,128)(2,1)} %copy-done, f32[1,1,1024,1024]{2,3,1,0:T(8,128)S(1)} %copy-done.1), kind=kOutput, calls=%fused_computation.8 | convolution fusion | flops 2152725504 | bytes 10489856 | tf_op jit(solution)/shard_map/bnm,bkm->bnk/dot_general | solution.py:87
  208.2 0.6 reduce_max.19
  209.5 1.5 fusion.45
  211.1 5.1 %fusion.29 = bf16[128,1024]{1,0:T(8,128)(2,1)S(1)} fusion(f32[1024,1024]{0,1:T(8,128)} %get-tuple-element.10, f32[]{:T(128)S(6)} %div.20, bf16[128,1024]{1,0:T(8,128)(2,1)S(1)} %fusion.45, s32[128]{0:T(128)S(1)} %iota_add_fusion), kind=kOutput, calls=%fused_computation.23 | convolution fusion | flops 543817728 | bytes 4719108 | tf_op jit(solution)/shard_map/bij,bjk->bik/dot_general | solution.py:44
  216.3 3.3 fusion.48
  219.6 3.0 fusion.43
  222.7 3.0 fusion.41
  225.7 5.0 %fusion.34 = bf16[128,1024]{1,0:T(8,128)(2,1)S(1)} fusion(bf16[128,1024]{1,0:T(8,128)(2,1)S(1)} %fusion.41, f32[1024,1024]{0,1:T(8,128)} %get-tuple-element.8, f32[]{:T(128)S(6)} %div.21), kind=kOutput, calls=%fused_computation.25 | convolution fusion | flops 547356672 | bytes 4718596 | tf_op jit(solution)/shard_map/bij,bjk->bik/dot_general | solution.py:44
  230.7 5.7 %multiply_reduce_fusion = (f32[]{:T(128)}, f32[128,1024]{1,0:T(8,128)S(1)}) fusion(f32[]{:T(128)S(6)} %mul.123, f32[1024,1024]{0,1:T(8,128)} %get-tuple-element.8, f32[]{:T(128)S(6)} %div.21, bf16[128,1024]{1,0:T(8,128)(2,1)S(1)} %fusion.34, f32[128,1024]{1,0:T(8,128)S(1)} %fusion.43), kind=kOutput, calls=%fused_computation.35 | convolution fusion | flops 543817728 | bytes 5505036 | tf_op jit(solution)/shard_map/bij,bjk->bik/dot_general | solution.py:44
  236.4 0.6 broadcast_in_dim.30
  237.1 8.8 %all_to_all.71 = f32[8,1,1]{2,1,0:T(1,128)S(1)} all-to-all(f32[8,1,1]{2,1,0:T(1,128)S(1)} %broadcast_in_dim.30), channel_id=1, replica_groups=mesh['batch'=8,'hidden'=4,'solver'=8] {'solver'}, dimensions={0} | all-to-all | bytes 64 | tf_op jit(solution)/shard_map/all_to_all | solution.py:20
  245.9 6.1 %all-to-all-start.1 = ((bf16[128,32,256]{0,2,1:T(8,128)(2,1)}), bf16[128,32,256]{0,2,1:T(8,128)(2,1)S(1)}, u32[]{:S(2)}, u32[]{:S(2)}) async-start(bf16[128,32,256]{0,2,1:T(8,128)(2,1)} %bitcast.1), calls=%async_computation.1 | async-start | bytes 4194304 | tf_op jit(solution)/shard_map/all_to_all | solution.py:66
  252.0 0.6 reduce_sum.52
  253.3 0.9 subtract_convert_fusion
  254.2 0.2 copy.50
  254.4 47.3 %all-to-all-done.1 = bf16[128,32,256]{0,2,1:T(8,128)(2,1)S(1)} async-done(((bf16[128,32,256]{0,2,1:T(8,128)(2,1)}), bf16[128,32,256]{0,2,1:T(8,128)(2,1)S(1)}, u32[]{:S(2)}, u32[]{:S(2)}) %all-to-all-start.1) | async-done | bytes 2097184 | tf_op jit(solution)/shard_map/all_to_all | solution.py:66
  301.7 1.6 broadcast_in_dim.31
  303.3 4.5 %all-to-all-start.6 = ((bf16[8,128,1024]{1,2,0:T(8,128)(2,1)}), bf16[8,128,1024]{1,2,0:T(8,128)(2,1)}, u32[]{:S(2)}, u32[]{:S(2)}) async-start(bf16[8,128,1024]{1,2,0:T(8,128)(2,1)} %broadcast_in_dim.31), calls=%async_computation.6 | async-start | bytes 4194304 | tf_op jit(solution)/shard_map/all_to_all | solution.py:20
  307.7 0.0 all-gather.2.cloned.1.call-start
  307.8 0.7 all-gather.2.cloned.1.call-update
  308.5 26.6 %all-to-all-done.6 = bf16[8,128,1024]{1,2,0:T(8,128)(2,1)} async-done(((bf16[8,128,1024]{1,2,0:T(8,128)(2,1)}), bf16[8,128,1024]{1,2,0:T(8,128)(2,1)}, u32[]{:S(2)}, u32[]{:S(2)}) %all-to-all-start.6) | async-done | bytes 2097184 | tf_op jit(solution)/shard_map/all_to_all | solution.py:20
  335.0 5.6 %all-to-all-start.7 = ((bf16[128,32,256]{0,2,1:T(8,128)(2,1)}), bf16[128,32,256]{0,2,1:T(8,128)(2,1)}, u32[]{:S(2)}, u32[]{:S(2)}) async-start(bf16[128,32,256]{0,2,1:T(8,128)(2,1)} %bitcast.17), calls=%async_computation.7 | async-start | bytes 4194304 | tf_op jit(solution)/shard_map/all_to_all | solution.py:122
  340.7 2.9 copy.42
  343.6 61.8 %all-gather.2.cloned.1.call-done = bf16[256,4096]{1,0:T(8,128)(2,1)} async-done(((bf16[256,128]{1,0:T(8,128)(2,1)}), bf16[256,4096]{1,0:T(8,128)(2,1)}) %all-gather.2.cloned.1.call-update) | async-done | bytes 2097168 | tf_op jit(solution)/shard_map/all_gather | solution.py:65
  405.4 3.6 convolution_convert_fusion.2
  409.0 1.3 constant_dynamic-slice_fusion
  410.3 1.0 copy.48
  411.3 1.0 copy.46
  412.3 3.3 copy.51
  415.6 3.0 convolution_convert_fusion.1
  (12 shorter events, 0.0 us)
Async XLA Ops:
  8.5 106.9 %copy-start.4 = (bf16[256,128]{1,0:T(8,128)(2,1)S(1)}, bf16[256,128]{1,0:T(8,128)(2,1)}, u32[]{:S(2)}) copy-start(bf16[256,128]{1,0:T(8,128)(2,1)} %param.5) | copy-start | bytes 196612
  148.3 6.9 %copy-start.3 = (bf16[128,1024]{1,0:T(8,128)(2,1)S(1)}, bf16[128,1024]{1,0:T(8,128)(2,1)}, u32[]{:S(2)}) copy-start(bf16[128,1024]{1,0:T(8,128)(2,1)} %param.7) | copy-start | bytes 786436
  150.3 29.2 %all-to-all-start.4 = ((bf16[8,1,1024,128]{3,2,1,0:T(8,128)(2,1)}), bf16[8,1,1024,128]{3,2,1,0:T(8,128)(2,1)S(1)}, u32[]{:S(2)}, u32[]{:S(2)}) async-start(bf16[8,1,1024,128]{3,2,1,0:T(8,128)(2,1)} %broadcast_in_dim.13), calls=%async_computation.4 | async-start | bytes 4194304 | tf_op jit(solution)/shard_map/all_to_all | solution.py:20
  179.5 9.0 %copy-start = (bf16[8,1,1024,128]{3,2,1,0:T(8,128)(2,1)}, bf16[8,1,1024,128]{3,2,1,0:T(8,128)(2,1)S(1)}, u32[]{:S(2)}) copy-start(bf16[8,1,1024,128]{3,2,1,0:T(8,128)(2,1)S(1)} %all-to-all-done.4) | copy-start | bytes 6291460
  181.3 55.1 %all-to-all-start = ((bf16[8,128,1024]{1,2,0:T(8,128)(2,1)}), bf16[8,128,1024]{1,2,0:T(8,128)(2,1)}, u32[]{:S(2)}, u32[]{:S(2)}) async-start(bf16[8,128,1024]{1,2,0:T(8,128)(2,1)} %broadcast_in_dim.12), calls=%async_computation | async-start | bytes 4194304 | tf_op jit(solution)/shard_map/all_to_all | solution.py:20
  198.0 3.5 copy-start.1
  211.1 5.2 %copy-start.2 = (bf16[1,1024,8,128]{1,3,2,0:T(8,128)(2,1)S(1)}, bf16[1,1024,8,128]{1,3,2,0:T(8,128)(2,1)}, u32[]{:S(2)}) copy-start(bf16[1,1024,8,128]{1,3,2,0:T(8,128)(2,1)} %copy.45) | copy-start | bytes 6291460
  245.9 55.8 %all-to-all-start.1 = ((bf16[128,32,256]{0,2,1:T(8,128)(2,1)}), bf16[128,32,256]{0,2,1:T(8,128)(2,1)S(1)}, u32[]{:S(2)}, u32[]{:S(2)}) async-start(bf16[128,32,256]{0,2,1:T(8,128)(2,1)} %bitcast.1), calls=%async_computation.1 | async-start | bytes 4194304 | tf_op jit(solution)/shard_map/all_to_all | solution.py:66
  303.3 31.8 %all-to-all-start.6 = ((bf16[8,128,1024]{1,2,0:T(8,128)(2,1)}), bf16[8,128,1024]{1,2,0:T(8,128)(2,1)}, u32[]{:S(2)}, u32[]{:S(2)}) async-start(bf16[8,128,1024]{1,2,0:T(8,128)(2,1)} %broadcast_in_dim.31), calls=%async_computation.6 | async-start | bytes 4194304 | tf_op jit(solution)/shard_map/all_to_all | solution.py:20
  307.7 97.7 %all-gather.2.cloned.1.call-start = ((), (), s32[]{:S(2)}) async-start(), calls=%async_computation.8 | async-start | bytes 2162688 | tf_op jit(solution)/shard_map/all_gather | solution.py:65
  335.0 77.3 %all-to-all-start.7 = ((bf16[128,32,256]{0,2,1:T(8,128)(2,1)}), bf16[128,32,256]{0,2,1:T(8,128)(2,1)}, u32[]{:S(2)}, u32[]{:S(2)}) async-start(bf16[128,32,256]{0,2,1:T(8,128)(2,1)} %bitcast.17), calls=%async_computation.7 | async-start | bytes 4194304 | tf_op jit(solution)/shard_map/all_to_all | solution.py:122
Sparse Core Ops, SparseCore 0:
  311.0 94.3 all-gather.1
